TPU v7x, 32 devices: a whole 2x2x4 slice. The times are simulated.
32 devices in a mesh: grp: 2 (over y), tm: 8 (over z, x), unit: 2 (over core).
Axes of the slice: x: 2, y: 2, z: 4, core: 2. Of those that a mesh axis runs over, the one named last changes fastest.
Arguments:
- panel_data: bfloat16 [1024, 64], P(('grp', 'tm', 'unit')), parts along dimension 0, may hold values from -6 to 6
- cell_mask: int32 [8, 64], P('grp'), parts along dimension 0, may hold values 0 or 1
- loadings: bfloat16 [512, 128], replicated, may hold values from -1 to 1
- noise_prec: float32 [512], replicated, may hold values from 0.5 to 4
- transition: float32 [128, 128], replicated, may hold values from -1 to 1, as said below
- proc_var: float32 [128], replicated, may hold values from 0.00625 to 2
- prior_mean: float32 [128], replicated, may hold values from -6 to 6
Outputs:
- smoothed_mean: float32 [128, 128], P(('grp', 'tm')), parts along dimension 0
- smoothed_var: float32 [128, 128], P(('grp', 'tm')), parts along dimension 0
There are 2 independent parts, one for each index of `grp`. A program takes and returns all parts, laid end to end along the dimension named above; an argument that names none is the same for every part. Nothing has to cross between parts.
Inputs may be any that keep to these rules, and one draw needn't show every extreme that they name: transition is lower triangular with diagonal entries in (0, 1).
All inputs are finite; a program needn't handle non-finite values.
Results may differ from a plain program's by a relative error of at most 0.003.
Values may be sent and summed in bfloat16 or wider, within the bound.
No kernel may reach another device: no remote copies, remote signals or barrier semaphores. Data moves between devices by JAX's collectives and lax.ppermute only.
A program may use at most 128 MiB of HBM per device.

v0:
```python
import functools

import jax
import jax.numpy as jnp
from jax import lax
from jax.experimental import pallas as pl
from jax.experimental.pallas import tpu as pltpu
from jax.sharding import PartitionSpec as P

f32 = jnp.float32
bf16 = jnp.bfloat16
WIDTH = 128
HIGHEST = lax.Precision.HIGHEST
VMEM_LIMIT = 30 << 20
RESIDUAL_MAX = 7e-3
GROUP = 16
JOIN_BOUNDS = ((1.0, 4.0), (1.0, 5.2), (1.0, 5.2), (1.0, 6.0), (1.0, 10.0), (1.0, 13.0))
COV_BOUNDS = ((0.70, 1.37), (0.50, 1.90), (0.31, 2.85), (0.19, 4.50), (0.12, 6.30))


def schedule(bounds, goal=2.5e-3):
    low, high = bounds
    alpha, radius, factors = 2.0 / (low + high), (high - low) / (high + low), []
    while radius > goal:
        square = radius * radius
        factors.append(2.0 / (2.0 - square))
        radius = square / (2.0 - square)
    return alpha, factors


def bounds_at(table, level):
    return table[min(level, len(table) - 1)]


def mm(left, right):
    return lax.dot_general(left, right, (((1,), (0,)), ((), ())), preferred_element_type=f32)


def mm_nt(left, right):
    return lax.dot_general(left, right, (((1,), (1,)), ((), ())), preferred_element_type=f32)


def split(value):
    high = value.astype(bf16)
    return high, (value - high.astype(f32)).astype(bf16)


def lanes(*parts):
    return jnp.concatenate(parts, axis=1)


def rows(*parts):
    return jnp.concatenate(parts, axis=0)


def mm3(left, right):
    lh, ll = split(left)
    rh, rl = split(right)
    return mm(lanes(lh, ll), rows(rh, rh)) + mm(lh, rl)


def mm3_nt(left, right):
    lh, ll = split(left)
    rh, rl = split(right)
    return mm_nt(lanes(lh, ll), lanes(rh, rh)) + mm_nt(lh, rl)


def identity():
    shape = (WIDTH, WIDTH)
    return (lax.broadcasted_iota(jnp.int32, shape, 0) == lax.broadcasted_iota(jnp.int32, shape, 1)).astype(f32)


def squares(value):
    return jnp.sum((value * value).reshape(WIDTH // 8, 8, WIDTH), axis=0)


def fast_inverses(items, eye, beside=iter(())):
    mats = [mat for mat, _, _ in items]
    plans = [schedule(bounds) for _, bounds, _ in items]
    n = range(len(items))
    halves = [split(mat) for mat in mats]
    rest = [eye - plan[0] * mat for plan, mat in zip(plans, mats)]
    guess = [(plan[0] * plan[1][0]) * (eye + r) for plan, r in zip(plans, rest)]
    for step in range(max(len(factors) for _, factors in plans)):
        rest_b = [r.astype(bf16) for r in rest]
        guess_b = [g.astype(bf16) for g in guess]
        for k in n:
            factors = plans[k][1]
            more = step + 1 < len(factors)
            if step >= len(factors):
                continue
            factor = factors[step]
            if step == 0:
                if more:
                    rest[k] = (1.0 - factor) * eye + factor * mm(rest_b[k], rest_b[k])
            elif more:
                out = mm(rest_b[k], lanes(guess_b[k], rest_b[k]))
                guess[k] = factor * (guess[k] + out[:, :WIDTH])
                rest[k] = (1.0 - factor) * eye + factor * out[:, WIDTH:]
            else:
                guess[k] = factor * (guess[k] + mm(rest_b[k], guess_b[k]))
        next(beside, None)
    guess_b = [g.astype(bf16) for g in guess]
    resid = [eye - mm(lanes(h, l), rows(g, g)) for (h, l), g in zip(halves, guess_b)]
    guess = [g.astype(f32) + mm(g, e.astype(bf16)) for g, e in zip(guess_b, resid)]
    next(beside, None)
    sides = [(g, e.astype(bf16)) for g, e in zip(guess_b, resid)]
    again = [k for k in n if items[k][2]]
    fine = {k: eye - mm3(mats[k], guess[k]) for k in again}
    for k in again:
        resid[k] = fine[k]
        guess[k] = guess[k] + mm(guess[k].astype(bf16), fine[k].astype(bf16))
        sides[k] = (guess[k], None)
    worst = squares(resid[0])
    for e in resid[1:]:
        worst = jnp.maximum(worst, squares(e))
    return guess, sides, worst


def safe_inverse(mat, eye):
    size = jnp.max(jnp.sum(jnp.abs(mat), axis=0, keepdims=True), axis=1, keepdims=True)
    product = functools.partial(jnp.dot, precision=HIGHEST, preferred_element_type=f32)

    def unfinished(state):
        step, size, _ = state
        return jnp.logical_and(step < 64, jnp.logical_not(size <= 1e-7))

    def improve(state):
        step, _, guess = state
        resid = eye - product(mat, guess)
        return step + 1, jnp.sum(squares(resid)), guess + product(guess, resid)

    return lax.while_loop(unfinished, improve, (0, f32(jnp.inf), eye / size))[2]


def diagonal(mat, eye):
    return jnp.sum(mat * eye, axis=0, keepdims=True)


def scaled(mat, eye):
    row = 1.0 / diagonal(mat, eye)
    return mat * row, row


def pack(value):
    return lanes(*split(value))


def unpack(value):
    return value[:, :WIDTH].astype(f32) + value[:, WIDTH:].astype(f32)


def path_steps(half, steps, first):
    found = []
    for level in reversed(range(half.bit_length() - 1)):
        stride = 1 << level
        if 2 * stride > steps:
            found.append((level, (first // (2 * stride)) * (2 * stride) + stride - 1))
        else:
            found += [(level, first + (2 * k + 1) * stride - 1) for k in range(steps // (2 * stride))]
    return found


def join_item(level, pair, eye):
    (_, c1, _), (_, _, j2) = pair
    return eye + mm3(c1, j2), bounds_at(JOIN_BOUNDS, level), False


def in_turns(*works):
    works = list(works)
    while works:
        for work in tuple(works):
            if next(work, works) is works:
                works.remove(work)


def joining(level, pairs, inverses, eye, results):
    turned = [jnp.transpose(one[0]) for one, two in pairs]
    if level < 2:
        less = [(eye - p).astype(bf16) for p in inverses]
        us = [two[0] - mm(two[0].astype(bf16), d) for (one, two), d in zip(pairs, less)]
        vs = [one[0] - mm(d, one[0].astype(bf16)) for (one, two), d in zip(pairs, less)]
    else:
        us = [mm3(two[0], p) for (one, two), p in zip(pairs, inverses)]
        vs = [mm3(p, one[0]) for (one, two), p in zip(pairs, inverses)]
    yield
    zs = [mm3(u, one[1]) for u, (one, two) in zip(us, pairs)]
    ys = [mm3(two[2], v) for v, (one, two) in zip(vs, pairs)]
    yield
    ts = [mm3(two[0], v) for v, (one, two) in zip(vs, pairs)]
    few = level < 2
    cs = [
        two[1] + (mm_nt(z.astype(bf16), two[0].astype(bf16)) if few else mm3_nt(z, two[0]))
        for z, (one, two) in zip(zs, pairs)
    ]
    yield
    js = [one[2] + (mm(t.astype(bf16), y.astype(bf16)) if few else mm3(t, y)) for t, y, (one, two) in zip(turned, ys, pairs)]
    results += list(zip(us, vs, ts, zs, ys, cs, js))


def condition_item(level, entry, eye):
    mat, scale = scaled(entry["c"], eye)
    return (mat, bounds_at(COV_BOUNDS, level), level > 2), scale


def conditioning(entries, scales, inverses, results):
    zs, vs = [e["z"] for e in entries], [e["v"] for e in entries]
    kepts = [mm3(e["p"], e["c1"]) for e in entries]
    backs = [mm3(jnp.transpose(inverse) * scale, z) for inverse, scale, z in zip(inverses, scales, zs)]
    yield
    forths = [jnp.transpose(back) for back in backs]
    gains = [v - mm3(forth, e["a"]) for v, forth, e in zip(vs, forths, entries)]
    yield
    conds = [kept - mm3(forth, z) for kept, forth, z in zip(kepts, forths, zs)]
    yield
    results += [
        (
            pack(rows(jnp.transpose(gain), back)),
            cond,
            pack(rows(jnp.transpose(e["p"]), jnp.transpose(kept), -back)),
        )
        for e, gain, back, cond, kept in zip(entries, gains, backs, conds, kepts)
    ]


def level_entry(refs, level, node, c1):
    uz_ref, yv_ref, a_ref, c_ref, _, p_ref = refs
    uz = uz_ref[node]
    return dict(
        z=uz[:WIDTH, WIDTH:].astype(f32) + uz[WIDTH:, WIDTH:].astype(f32),
        v=unpack(yv_ref[node, WIDTH:, :]),
        a=a_ref[node],
        c=c_ref[node],
        p=p_ref[node],
        c1=c1,
    )


LEVEL_ARRAYS = 6


def first_kernel(half, index_ref, mask_hbm, load_hbm, prec_hbm, trans_hbm, var_hbm, prior_hbm,
                 weight_ref, end_ref, mask_out, const_ref, uz_ref, yv_ref, a_ref, c_ref, j_ref, p_ref,
                 gram_ref, acc_ref, mask_ref, mask_vmem, load_ref, prec_ref, base_ref, row_ref, sems):
    unit, n_unit = index_ref[0], index_ref[2]
    copies = [
        pltpu.make_async_copy(source, target, sems.at[k])
        for k, (source, target) in enumerate((
            (load_hbm, load_ref), (prec_hbm, prec_ref), (trans_hbm, base_ref.at[0]), (var_hbm, row_ref.at[0]),
            (prior_hbm, row_ref.at[1]), (mask_hbm, mask_ref), (mask_hbm, mask_vmem),
        ))
    ]
    for copy in copies:
        copy.start()
    for copy in copies:
        copy.wait()
    eye = identity()
    n_blocks = load_ref.shape[0] // WIDTH
    for block in range(n_blocks):
        load = load_ref[block * WIDTH:(block + 1) * WIDTH, :]
        weighted = (jnp.transpose(load.astype(f32)) * prec_ref[block:block + 1, :]).astype(bf16)
        weight_ref[block] = weighted
        gram = mm(weighted, load)
        gram_ref[block] = 0.5 * (gram + jnp.transpose(gram))
    base_ref[1] = eye * row_ref[0]
    base_ref[2] = jnp.transpose(base_ref[0])
    base_ref[3] = jnp.transpose(jnp.broadcast_to(row_ref[0], (WIDTH, WIDTH)))
    const_ref[0] = jnp.broadcast_to(row_ref[1], (WIDTH, WIDTH))
    const_ref[1] = base_ref[1]
    mask_out[...] = mask_vmem[...].astype(f32).astype(bf16)

    def info(step):
        out = mask_ref[0, step].astype(f32) * gram_ref[0]
        for block in range(1, n_blocks):
            out = out + mask_ref[block, step].astype(f32) * gram_ref[block]
        return out

    end_ref[...] = info(n_unit * half - 1)

    outs = (uz_ref, yv_ref, a_ref, c_ref, j_ref, p_ref)

    def leaf_joins(nodes, fast):
        trans, noise, turned, column, row = base_ref[0], base_ref[1], base_ref[2], base_ref[3], row_ref[0]
        step = [unit * half + 2 * node for node in nodes]
        start = jnp.where(step[0] == 0, 1.0, 0.0).astype(f32)
        before = [info(jnp.maximum(at - 1, 0)) for at in step]
        before[0] = before[0] * (1.0 - start)
        after = [info(at) for at in step]
        left = [trans * (1.0 - start)] + [trans] * (len(nodes) - 1)
        rows_of = [row + start * (1.0 - row)] + [row] * (len(nodes) - 1)
        mats = [eye + column * j for j in after]
        mats[0] = eye + (column + start * (1.0 - column)) * after[0]
        inverses = invert([(mat, bounds_at(JOIN_BOUNDS, 0), False) for mat in mats], eye, fast, acc_ref)
        less = [(eye - p).astype(bf16) for p in inverses]
        trans_b, turned_b = trans.astype(bf16), turned.astype(bf16)
        us = [trans - mm(trans_b, d) for d in less]
        vs = [one - mm(d, one.astype(bf16)) for one, d in zip(left, less)]
        zs = [u * r for u, r in zip(us, rows_of)]
        ts = [mm3(trans, v) for v in vs]
        ys = [mm3(j, v) for j, v in zip(after, vs)]
        cs = [noise + mm_nt(z.astype(bf16), trans_b) for z in zs]
        js = [j + mm(turned_b, y.astype(bf16)) for j, y in zip(before, ys)]
        for node, p, u, v, t, z, y, c, j in zip(nodes, inverses, us, vs, ts, zs, ys, cs, js):
            zh, zl = split(z)
            uz_ref[node, :, WIDTH:] = rows(zh, zl)
            yv_ref[node, WIDTH:, :] = pack(v)
            p_ref[node] = p
            a_ref[node] = t
            c_ref[node] = c
            j_ref[node] = j
        uh, ul = split(us[0])
        uz_ref[nodes[0], :, :WIDTH] = rows(uh, ul)
        yv_ref[nodes[0], :WIDTH, :] = pack(ys[0])

    def sweep(fast):
        count = half // 2
        group = min(count, GROUP) if fast else 1

        def some(block, carry):
            leaf_joins([block * group + k for k in range(group)], fast)
            return carry

        lax.fori_loop(0, count // group, some, 0)

    checked(sweep, acc_ref)


def invert(items, eye, fast, acc_ref, apart=False, beside=iter(())):
    if not fast:
        inverses = [safe_inverse(mat, eye) for mat, _, _ in items]
        return (inverses, [(p, None, None) for p in inverses]) if apart else inverses
    inverses, sides, worst = fast_inverses(items, eye, beside)
    acc_ref[...] = jnp.maximum(acc_ref[...], worst)
    return (inverses, [(g, e, mat) for (g, e), (mat, _, _) in zip(sides, items)]) if apart else inverses


def times_inverse(left, side):
    guess, resid, _ = side
    if resid is None:
        return mm3(left, guess)
    out = mm(lanes(*split(left)), rows(guess, guess))
    return out + mm(out.astype(bf16), resid)


def inverse_times(side, right, eye):
    guess, resid, mat = side
    if resid is None:
        return mm3(guess, right)
    resid = eye - mm(lanes(guess, guess), rows(*split(mat)))
    out = mm(lanes(guess, guess), rows(*split(right)))
    return out + mm(resid.astype(bf16), out.astype(bf16))


def checked(sweep, acc_ref, **beside):
    acc_ref[...] = jnp.zeros((8, WIDTH), f32)
    sweep(True, **beside)
    worst = jnp.sum(acc_ref[...])

    @pl.when(jnp.logical_not(worst <= RESIDUAL_MAX))
    def _():
        sweep(False)


def store_joined(outs, nodes, inverses, results):
    uz_ref, yv_ref, a_ref, c_ref, j_ref, p_ref = outs
    for node, p, (u, v, t, z, y, c, j) in zip(nodes, inverses, results):
        uh, ul = split(u)
        zh, zl = split(z)
        uz_ref[node] = rows(lanes(uh, zh), lanes(ul, zl))
        yv_ref[node] = rows(pack(y), pack(v))
        p_ref[node] = p
        a_ref[node] = t
        c_ref[node] = c
        j_ref[node] = j


def entries_of(level, half, steps, first, unit, refs, below):
    found = []
    for at_level, at in path_steps(half, steps, first):
        if at_level != level:
            continue
        node = at // (2 << level)
        if level == 0:
            eye = identity()
            start = jnp.where(unit * half + at == 0, 1.0, 0.0).astype(f32)
            c1 = below + start * (eye - below)
        else:
            c1 = below[2 * node]
        found.append(level_entry(refs, level, node, c1))
    return found


def panel_vectors(half, rows_own, unit, place, panel_in, mask_ref, weight_ref, panel_ref, all_ref, leaf_ref):
    total = panel_ref.shape[1]
    n_blocks = weight_ref.shape[0]
    n_time = panel_in.shape[0] // (2 * rows_own)
    for k in range(2 * n_time):
        core, chip, hop = (1 - unit if k % 2 else unit), place, n_time // 2
        for bit in range(1, n_time.bit_length()):
            if (k >> bit) % 2:
                chip = jnp.bitwise_xor(chip, hop)
            hop = hop // 2
        at = pl.multiple_of((2 * chip + core) * rows_own, rows_own)
        panel_ref[pl.ds(at, rows_own), :] = panel_in[k * rows_own:(k + 1) * rows_own, :]
    turned = jnp.zeros((WIDTH, total), f32)
    for block in range(n_blocks):
        mask = mask_ref[block:block + 1, :]
        turned = turned + mm(weight_ref[block], mask * panel_ref[block * WIDTH:(block + 1) * WIDTH, :])
    late = pltpu.roll(jnp.transpose(turned), 1, 0)
    all_ref[...] = late
    all_ref[0:1, :] = jnp.zeros((1, WIDTH), f32)
    leaf = all_ref[pl.ds(pl.multiple_of(unit * half, half), half), :]
    leaf_ref[...] = leaf
    return late[0:1, :], leaf


def vector_level(level, half, prior, gain_refs, leaf, bs, es):
    uz_ref, yv_ref = gain_refs
    stride = 1 << level
    zero = jnp.zeros((1, WIDTH), f32)
    for node in range(half >> (level + 1)):
        if node and node % 4 == 0:
            yield
        at = (2 * node + 1) * stride - 1
        if level == 0:
            b1, b2 = (prior if node == 0 else zero), zero
            e1, e2 = leaf[at:at + 1, :], leaf[at + 1:at + 2, :]
            if node > 0:
                high, low = split(e2)
                both = rows(high, low)
                out = mm_nt(both, uz_ref[node, :, WIDTH:])
                bs[at] = out[0:1, :WIDTH] + out[1:2, :WIDTH] + out[0:1, WIDTH:]
                out = mm(both, yv_ref[node, WIDTH:, :])
                es[at] = e1 + out[0:1, :WIDTH] + out[1:2, :WIDTH] + out[0:1, WIDTH:]
                continue
        else:
            one, two = at - stride // 2, at + stride // 2
            b1, b2, e1, e2 = bs[one], bs[two], es[one], es[two]
        high, low = split(lanes(b1, e2))
        out = mm_nt(rows(high, low), uz_ref[node])
        bs[at] = b2 + out[0:1, :WIDTH] + out[1:2, :WIDTH] + out[0:1, WIDTH:]
        high, low = split(lanes(-b1, e2))
        out = mm(rows(high, low), yv_ref[node])
        es[at] = e1 + out[0:1, :WIDTH] + out[1:2, :WIDTH] + out[0:1, WIDTH:]


def up_kernel(joins, half, steps, rows_own, index_ref, const_ref, *refs):
    unit, place = index_ref[0], index_ref[1]
    n_levels = half.bit_length() - 1
    low = joins[0]
    held = {}
    refs = list(refs)
    if rows_own:
        panel_in, mask_ref, weight_ref = refs[:3]
        refs = refs[3:]
        gain_refs, refs = refs[:2 * (low - 1)], refs[2 * (low - 1):]
        panel_ref, all_ref = refs[-2:]
        leaf_ref, b_ref, e_ref, message_ref = refs[-7:-3]
        refs = refs[:-7] + refs[-3:-2]
    if low > 1:
        below_ref = refs.pop(0)
    held[low - 1], refs = refs[:LEVEL_ARRAYS], refs[LEVEL_ARRAYS:]
    outs = {}
    for level in joins:
        held[level], refs = refs[:LEVEL_ARRAYS], refs[LEVEL_ARRAYS:]
        outs[level], refs = refs[:3], refs[3:]
    acc_ref, = refs
    eye = identity()

    def children(level, node):
        _, _, a_ref, c_ref, j_ref, _ = held[level - 1]
        return tuple((a_ref[k], c_ref[k], j_ref[k]) for k in (2 * node, 2 * node + 1))

    def condition_inputs(level):
        if level == 0:
            below = const_ref[1]
        elif level == low - 1:
            below = below_ref
        else:
            below = held[level - 1][3]
        return entries_of(level, half, steps, place * steps, unit, held[level], below)

    def store(level, results):
        for slot, result in enumerate(results):
            for ref, value in zip(outs[level], result):
                ref[slot] = value

    def sweep(fast, beside=iter(())):
        for level in joins:
            count = half >> (level + 1)
            under = level - 1
            if fast and count <= GROUP:
                nodes = list(range(count))
                entries = condition_inputs(under)
                pairs = [children(level, node) for node in nodes]
                items = [join_item(level, pair, eye) for pair in pairs]
                extra = [condition_item(under, entry, eye) for entry in entries]
                inverses = invert(items + [item for item, _ in extra], eye, True, acc_ref, beside=beside)
                results, seen = [], []
                in_turns(
                    joining(level, pairs, inverses[:count], eye, results),
                    conditioning(entries, [scale for _, scale in extra], inverses[count:], seen),
                    beside,
                )
                store_joined(held[level], nodes, inverses[:count], results)
                store(level, seen)
                continue
            group = min(count, GROUP) if fast else 1

            def some(block, carry):
                nodes = [block * group + k for k in range(group)]
                pairs = [children(level, node) for node in nodes]
                inverses = invert([join_item(level, pair, eye) for pair in pairs], eye, fast, acc_ref)
                results = []
                in_turns(joining(level, pairs, inverses, eye, results))
                store_joined(held[level], nodes, inverses, results)
                return carry

            lax.fori_loop(0, count // group, some, 0)
            entries = condition_inputs(under)
            extra = [condition_item(under, entry, eye) for entry in entries]
            inverses = invert([item for item, _ in extra], eye, fast, acc_ref)
            seen = []
            in_turns(conditioning(entries, [scale for _, scale in extra], inverses, seen))
            store(level, seen)

    if not rows_own:
        checked(sweep, acc_ref)
        return
    prior = jnp.where(unit == 0, 1.0, 0.0) * const_ref[0, 0:1, :]
    gains = [gain_refs[2 * level:2 * level + 2] for level in range(low - 1)] + [held[low - 1][:2]]
    bs, es, found = {}, {}, []

    def means():
        found.extend(panel_vectors(
            half, rows_own, unit, index_ref[3], panel_in, mask_ref, weight_ref, panel_ref, all_ref, leaf_ref
        ))
        yield
        for level in range(low):
            yield from vector_level(level, half, prior, gains[level], found[1], bs, es)
            yield

    pieces = means()
    checked(sweep, acc_ref, beside=pieces)
    for _ in pieces:
        pass
    end, leaf = found
    for level in range(low, n_levels):
        in_turns(vector_level(level, half, prior, held[level][:2], leaf, bs, es))
    for at in bs:
        b_ref[at:at + 1, :] = bs[at]
        e_ref[at:at + 1, :] = es[at]
    top = half // 2 - 1
    _, _, a_ref, c_ref, j_ref, _ = held[n_levels - 1]
    for k, ref in enumerate((a_ref, c_ref, j_ref)):
        message_ref[k * WIDTH:(k + 1) * WIDTH, :] = ref[0]
    message_ref[3 * WIDTH:, :] = rows(bs[top], es[top], end, jnp.zeros((5, WIDTH), f32))


SMEM = pl.BlockSpec(memory_space=pltpu.SMEM)
VMEM = pl.BlockSpec(memory_space=pltpu.VMEM)


ANY = pl.BlockSpec(memory_space=pl.ANY)


def level_shapes(half, level):
    count = half >> (level + 1)
    mat = (count, WIDTH, WIDTH)
    wide = (count, 2 * WIDTH, 2 * WIDTH)
    return [jax.ShapeDtypeStruct(wide, bf16)] * 2 + [jax.ShapeDtypeStruct(mat, f32)] * 4


def path_shapes(half, steps, level):
    count = len([k for k, _ in path_steps(half, steps, 0) if k == level])
    return [
        jax.ShapeDtypeStruct((count, 2 * WIDTH, 2 * WIDTH), bf16),
        jax.ShapeDtypeStruct((count, WIDTH, WIDTH), f32),
        jax.ShapeDtypeStruct((count, 3 * WIDTH, 2 * WIDTH), bf16),
    ]


def estimate(matrices):
    return pl.CostEstimate(flops=matrices * 600 * WIDTH**3, transcendentals=0, bytes_accessed=1 << 20)


def first_sweep(half, index, cell_mask, loadings, prec_rows, transition, var_row, prior_row):
    mat = (WIDTH, WIDTH)
    n_blocks = loadings.shape[0] // WIDTH
    outs = [
        jax.ShapeDtypeStruct((n_blocks,) + mat, bf16),
        jax.ShapeDtypeStruct(mat, f32),
        jax.ShapeDtypeStruct(cell_mask.shape, bf16),
        jax.ShapeDtypeStruct((2,) + mat, f32),
    ] + level_shapes(half, 0)
    inputs = [
        pltpu.with_memory_space_constraint(array, pltpu.HBM)
        for array in (cell_mask, loadings, prec_rows, transition, var_row, prior_row)
    ]
    return pl.pallas_call(
        functools.partial(first_kernel, half),
        out_shape=outs,
        in_specs=[SMEM] + [ANY] * 6,
        out_specs=[VMEM] * len(outs),
        scratch_shapes=[
            pltpu.VMEM((n_blocks,) + mat, f32),
            pltpu.VMEM((8, WIDTH), f32),
            pltpu.SMEM(cell_mask.shape, jnp.int32),
            pltpu.VMEM(cell_mask.shape, jnp.int32),
            pltpu.VMEM(loadings.shape, bf16),
            pltpu.VMEM(prec_rows.shape, f32),
            pltpu.VMEM((4,) + mat, f32),
            pltpu.VMEM((2, 1, WIDTH), f32),
            pltpu.SemaphoreType.DMA((7,)),
        ],
        compiler_params=pltpu.CompilerParams(vmem_limit_bytes=VMEM_LIMIT),
        cost_estimate=estimate(half // 2),
        name="first_sweep",
    )(index, *inputs)


def up_sweep(joins, half, steps, index, consts, held, rows_own=0, vectors=()):
    low = joins[0]
    operands = ([held[low - 2][3]] if low > 1 else []) + list(held[low - 1])
    outs = []
    for level in joins:
        outs += level_shapes(half, level) + path_shapes(half, steps, level - 1)
    scratch = [pltpu.VMEM((8, WIDTH), f32)]
    if rows_own:
        panel = vectors[0]
        operands = list(vectors) + [array for level in held[:-1] for array in level[:2]] + operands
        row = jax.ShapeDtypeStruct((half, WIDTH), f32)
        outs += [row, row, row, jax.ShapeDtypeStruct((3 * WIDTH + 8, WIDTH), f32)]
        scratch += [pltpu.VMEM((panel.shape[1], WIDTH), f32)]
        scratch = scratch[:1] + [pltpu.VMEM(panel.shape, bf16)] + scratch[1:]
    results = pl.pallas_call(
        functools.partial(up_kernel, joins, half, steps, rows_own),
        out_shape=outs,
        in_specs=[SMEM] + [VMEM] * (1 + len(operands)),
        out_specs=[VMEM] * len(outs),
        scratch_shapes=scratch,
        compiler_params=pltpu.CompilerParams(vmem_limit_bytes=VMEM_LIMIT),
        cost_estimate=estimate(sum(half >> level for level in joins)),
        name="up_sweep_%d" % low,
    )(index, consts, *operands)
    results = list(results)
    step = LEVEL_ARRAYS + 3
    parts = [results[k * step:(k + 1) * step] for k in range(len(joins))]
    return [part[:LEVEL_ARRAYS] for part in parts], [part[LEVEL_ARRAYS:] for part in parts], results[len(joins) * step:]


def down_kernel(steps, index_ref, own_ref, other_ref, end_ref, const_ref, leaf_ref, b_ref, e_ref, below_ref,
                *refs):
    refs = list(refs)
    top_refs, refs = refs[:LEVEL_ARRAYS], refs[LEVEL_ARRAYS:]
    out_ref, acc_ref, top_ref, gt_ref, cond_ref, shift_ref = refs[-6:]
    path_refs = refs[:-6]
    unit, place = index_ref[0], index_ref[1]
    half = leaf_ref.shape[0]
    n_levels = half.bit_length() - 1
    eye = identity()
    flag = jnp.where(unit == 0, 1.0, 0.0).astype(f32)

    def pick(zero, one):
        return flag * zero + (1.0 - flag) * one

    def both(first, count):
        part = slice(first, first + count)
        return own_ref[part, :], other_ref[part, :]

    own, other = both(WIDTH, WIDTH)
    cov0 = pick(own, other)
    trans1, cov1, info1 = [pick(*both(k * WIDTH, WIDTH)[::-1]) for k in range(3)]
    b0 = pick(*both(3 * WIDTH, 1))
    b1, e1 = [pick(*both(3 * WIDTH + k, 1)[::-1]) for k in range(2)]
    e_end = own_ref[3 * WIDTH + 2:3 * WIDTH + 3, :]
    end = end_ref[...]

    first = place * steps

    def roots(fast, beside=iter(())):
        under = n_levels - 1
        entries = entries_of(under, half, steps, first, unit, top_refs, below_ref)
        extra = [condition_item(under, entry, eye) for entry in entries]
        item = (eye + mm3(cov0, info1), bounds_at(JOIN_BOUNDS, n_levels), True)
        ready = mm3_nt(cov0, trans1)
        ready_end, cov1_end = mm3(ready, end), mm3(cov1, end)
        (p, *inverses), sides = invert([item] + [item for item, _ in extra], eye, fast, acc_ref, True, beside)
        u = times_inverse(trans1, sides[0])
        last = eye + cov1_end + mm3(u, ready_end)
        cov = cov1 + mm3(u, ready)
        z = mm3(u, cov0)
        kept = mm3(p, cov0)
        results = []
        in_turns(conditioning(entries, [scale for _, scale in extra], inverses, results), beside)
        for slot, result in enumerate(results):
            for ref, value in zip((gt_ref, cond_ref, shift_ref), result):
                ref[slot] = value
        info_z = mm3(jnp.transpose(z), end)
        _, (side,) = invert([(last, bounds_at(JOIN_BOUNDS, 0), False)], eye, fast, acc_ref, True)
        top_ref[0], top_ref[1] = inverse_times(side, cov, eye), inverse_times(side, z, eye)
        top_ref[2] = kept - mm3(info_z, top_ref[1])
        top_ref[3] = p

    prior = flag * const_ref[0, 0:1, :]
    path = path_steps(half, steps, first)
    levels = [(gt_ref, cond_ref, shift_ref)] + [path_refs[k:k + 3] for k in range(0, len(path_refs), 3)]
    places, seen = [], {}
    for level, _ in path:
        seen[level] = seen.get(level, -1) + 1
        places.append((levels[n_levels - 1 - level], seen[level]))

    def shift(slot):
        level, at = path[slot]
        row_of = lambda ref, k: ref[pl.ds(k, 1), :]
        if level == 0:
            one, two = jnp.where(at == 0, 1.0, 0.0) * prior, row_of(leaf_ref, at + 1)
        else:
            near = (1 << level) // 2
            one, two = row_of(b_ref, at - near), row_of(e_ref, at + near)
        high, low = split(lanes(one, two, row_of(b_ref, at)))
        arrays, own = places[slot]
        out = mm(rows(high, low), arrays[2][own])
        return out[0:1, :WIDTH] + out[1:2, :WIDTH] + out[0:1, WIDTH:]

    shifts = {}

    def shifting():
        for slot, (level, _) in enumerate(path):
            if level < n_levels - 1:
                shifts[slot] = shift(slot)
                yield

    pieces = shifting()
    checked(roots, acc_ref, beside=pieces)
    for _ in pieces:
        pass
    shifts[0] = shift(0)
    cov_top, cov_cross, cov_mid, p = [top_ref[k] for k in range(4)]
    mean_mid = mm3_nt(b0 + mm3(e1, cov0), p)
    b_end = mm3_nt(mean_mid, trans1) + b1
    news = e_end - mm3(b_end, end)
    mean_top = b_end + mm3_nt(news, cov_top)
    mean_mid = mean_mid + mm3(news, cov_cross)
    keep = 1.0 - flag
    joint = rows(
        lanes(keep * cov_mid, keep * jnp.transpose(cov_cross)),
        lanes(keep * cov_cross, pick(cov_mid, cov_top)),
    )
    means = lanes(keep * mean_mid, pick(mean_mid, mean_top))

    def nodes(slots, joints, means, leaf):
        packs = [places[slot][0][0][places[slot][1]] for slot in slots]
        conds = [places[slot][0][1][places[slot][1]] for slot in slots]
        halves = [split(joint) for joint in joints]
        crosses = [
            mm(lanes(jh, jl), rows(g[:, :WIDTH], g[:, :WIDTH])) + mm(jh, g[:, WIDTH:])
            for (jh, jl), g in zip(halves, packs)
        ]
        outs = [mm(rows(*split(mean)), g) for mean, g in zip(means, packs)]
        found = [
            shifts[slot] + out[0:1, :WIDTH] + out[1:2, :WIDTH] + out[0:1, WIDTH:] for slot, out in zip(slots, outs)
        ]
        gains = [unpack(g) for g in packs]
        if leaf:
            owns = [
                diagonal(cond, eye) + jnp.sum(gain * cross, axis=0, keepdims=True)
                for cond, gain, cross in zip(conds, gains, crosses)
            ]
        else:
            owns = [cond + mm3(jnp.transpose(gain), cross) for cond, gain, cross in zip(conds, gains, crosses)]
        return list(zip(found, owns, crosses))

    def left_pair(joint, means, mean, own, cross):
        c = cross[:WIDTH]
        return rows(lanes(joint[:WIDTH, :WIDTH], c), lanes(jnp.transpose(c), own)), lanes(means[:, :WIDTH], mean)

    def right_pair(joint, means, mean, own, cross):
        c = cross[WIDTH:]
        return rows(lanes(own, jnp.transpose(c)), lanes(c, joint[WIDTH:, WIDTH:])), lanes(mean, means[:, WIDTH:])

    slot = 0
    while path[slot][0] >= steps.bit_length() - 1:
        result, = nodes([slot], [joint], [means], False)
        go_right = jnp.where(first > path[slot][1], 1.0, 0.0).astype(f32)
        lj, lm = left_pair(joint, means, *result)
        rj, rm = right_pair(joint, means, *result)
        joint = go_right * rj + (1.0 - go_right) * lj
        means = go_right * rm + (1.0 - go_right) * lm
        slot += 1

    out_ref[steps - 1:steps, :] = means[:, WIDTH:]
    out_ref[2 * steps - 1:2 * steps, :] = diagonal(joint[WIDTH:, WIDTH:], eye)
    todo = [(0, joint, means)]
    count = steps
    while todo:
        stride, later = count // 2, []
        leaf = stride == 1
        results = nodes(
            range(slot, slot + len(todo)), [joint for _, joint, _ in todo], [means for _, _, means in todo], leaf
        )
        slot += len(todo)
        for (low, joint, means), result in zip(todo, results):
            at = low + stride - 1
            out_ref[at:at + 1, :] = result[0]
            out_ref[steps + at:steps + at + 1, :] = result[1] if leaf else diagonal(result[1], eye)
            if not leaf:
                later.append((low,) + left_pair(joint, means, *result))
                later.append((low + stride,) + right_pair(joint, means, *result))
        todo, count = later, stride


def down_sweep(steps, half, *operands):
    return pl.pallas_call(
        functools.partial(down_kernel, steps),
        out_shape=jax.ShapeDtypeStruct((2 * steps, WIDTH), f32),
        in_specs=[SMEM] + [VMEM] * (len(operands) - 1),
        out_specs=VMEM,
        scratch_shapes=[pltpu.VMEM((8, WIDTH), f32), pltpu.VMEM((6, WIDTH, WIDTH), f32)]
        + [pltpu.VMEM(shape.shape, shape.dtype) for shape in path_shapes(half, steps, half.bit_length() - 2)],
        compiler_params=pltpu.CompilerParams(vmem_limit_bytes=VMEM_LIMIT),
        name="down_sweep",
    )(*operands)


def redundant(panel_data, cell_mask, loadings, noise_prec, transition, proc_var, prior_mean):
    n_time = lax.axis_size("tm")
    n_unit = lax.axis_size("unit")
    place, unit = lax.axis_index("tm"), lax.axis_index("unit")
    total = panel_data.shape[1]
    half = total // n_unit
    steps = total // n_time
    per_half = half // steps
    index = jnp.stack([unit, place % per_half, n_unit, place]).astype(jnp.int32)
    swap = [(0, 1), (1, 0)]

    def swapped(value, other):
        return lax.ppermute(value, "tm", [(k, k ^ other) for k in range(n_time)])

    n_levels = half.bit_length() - 1
    hops = [1 << k for k in reversed(range(n_time.bit_length() - 1))]
    weighted, end, mask, consts, *level0 = first_sweep(
        half, index, cell_mask, loadings, noise_prec.reshape(-1, WIDTH), transition,
        proc_var.reshape(1, WIDTH), prior_mean.reshape(1, WIDTH),
    )
    held, paths = [level0], []
    panel = jnp.concatenate([panel_data, lax.ppermute(panel_data, "unit", swap)])
    cuts = [[1], [2], [3], list(range(4, n_levels))]
    for k, joins in enumerate(cuts):
        panel, held[-1] = lax.optimization_barrier((panel, held[-1]))
        last = k + 1 == len(cuts)
        extra = (panel_data.shape[0], (panel, mask, weighted)) if last else ()
        new, path, rest = up_sweep(joins, half, steps, index, consts, held, *extra)
        if not last:
            panel = jnp.concatenate([panel, swapped(panel, hops[k])])
        held += new
        paths += path
    leaves, bs, es, message = rest
    other = lax.ppermute(message, "unit", swap)
    mine = down_sweep(
        steps, half, index, message, other, end, consts, leaves, bs, es, held[-2][3], *held[-1],
        *[array for path in reversed(paths) for array in path],
    )
    theirs = lax.ppermute(mine, "unit", swap)
    out = jnp.where(unit == place // per_half, mine, theirs)
    return out[:steps], out[steps:]


BLOCK = 128


def carried_in(value, axis, join, neutral, backward):
    count, mine = (lax.axis_size(axis), lax.axis_index(axis))
    pieces = jax.tree.map(lambda part: lax.all_gather(part, axis), value)
    if backward:
        pieces = jax.tree.map(lambda part: part[::-1], pieces)
        mine = count - 1 - mine
    running = jax.tree.map(
        lambda part, zero: jnp.full_like(part, 0) + jnp.asarray(zero, part.dtype), value, neutral
    )

    def step(position, running):
        longer = join(running, jax.tree.map(lambda part: part[position], pieces))
        return jax.tree.map(lambda new, old: jnp.where(position < mine, new, old), longer, running)

    return lax.fori_loop(0, count - 1, step, running)


def product(left, right):
    return jnp.matmul(left, right, precision=HIGHEST)


def mat_vec(matrix, vector):
    return jnp.einsum("...kl,...l->...k", matrix, vector, precision=HIGHEST)


def flipped(matrix):
    return jnp.swapaxes(matrix, -1, -2)


def chol_apply(factor, rhs):
    middle = lax.linalg.triangular_solve(factor, rhs, left_side=True, lower=True)
    return lax.linalg.triangular_solve(factor, middle, left_side=True, lower=True, transpose_a=True)


def filter_join(earlier, later):
    trans_one, shift_one, cov_one, info_one, vec_one, live_one = earlier
    trans_two, shift_two, cov_two, info_two, vec_two, live_two = later
    identity_mat = jnp.eye(trans_one.shape[-1], dtype=jnp.float32)
    live_mat = live_one[..., None, None]
    factor_one = jnp.linalg.cholesky(cov_one + (1.0 - live_mat) * identity_mat)
    inner_mat = identity_mat + product(product(flipped(factor_one), info_two), factor_one)
    inner_factor = jnp.linalg.cholesky(inner_mat)
    solved = lax.linalg.triangular_solve(
        inner_factor, flipped(factor_one), left_side=True, lower=True
    )
    spread_mat = product(trans_two, flipped(solved))
    pushed = product(info_two, trans_one)
    reduced = product(solved, pushed)
    residue = vec_two - mat_vec(info_two, shift_one)
    solved_residue = mat_vec(solved, residue)
    trans_new = product(trans_two, trans_one) - product(spread_mat, reduced)
    shift_new = mat_vec(trans_two, shift_one) + mat_vec(spread_mat, solved_residue) + shift_two
    cov_new = product(spread_mat, flipped(spread_mat)) + cov_two
    info_new = product(flipped(trans_one), pushed) - product(flipped(reduced), reduced) + info_one
    vec_new = (
        mat_vec(flipped(trans_one), residue) - mat_vec(flipped(reduced), solved_residue) + vec_one
    )
    alive_mat = live_mat > 0.5
    alive_vec = live_one[..., None] > 0.5
    return (
        jnp.where(alive_mat, trans_new, trans_two),
        jnp.where(alive_vec, shift_new, shift_two),
        jnp.where(alive_mat, cov_new, cov_two),
        jnp.where(alive_mat, info_new, info_two),
        jnp.where(alive_vec, vec_new, vec_two),
        jnp.maximum(live_one, live_two),
    )


def smooth_join(lower_elem, higher_elem):
    gain_low, offset_low, cov_low = lower_elem
    gain_high, offset_high, cov_high = higher_elem
    return (
        product(gain_low, gain_high),
        mat_vec(gain_low, offset_high) + offset_low,
        product(product(gain_low, cov_high), flipped(gain_low)) + cov_low,
    )


def smooth_scan_join(earlier, later):
    return smooth_join(later, earlier)


def take_last(stacked):
    return stacked[-1]


def take_first(stacked):
    return stacked[0]


def per_device(panel_data, cell_mask, loadings, noise_prec, transition, proc_var, prior_mean):
    n_time = lax.axis_size("tm")
    n_unit = lax.axis_size("unit")
    time_index = lax.axis_index("tm")
    unit_index = lax.axis_index("unit")
    rows_own, total_time = panel_data.shape
    steps = total_time // n_time
    width = transition.shape[0]
    identity_mat = jnp.eye(width, dtype=jnp.float32)
    my_columns = lax.dynamic_slice_in_dim(cell_mask, time_index * steps, steps, 1)
    half_load = lax.dynamic_index_in_dim(
        loadings.reshape(n_time, n_unit, rows_own, width), unit_index, 1, keepdims=False
    ).reshape(n_time * rows_own, width)
    half_prec = lax.dynamic_index_in_dim(
        noise_prec.reshape(n_time, n_unit, rows_own), unit_index, 1, keepdims=False
    ).reshape(n_time * rows_own)
    half_ids = (
        (jnp.arange(n_time, dtype=jnp.int32)[:, None] * n_unit + unit_index) * rows_own
        + jnp.arange(rows_own, dtype=jnp.int32)[None, :]
    ).reshape(-1)
    half_weighted = (half_prec[:, None] * half_load.astype(jnp.float32)).astype(jnp.bfloat16)
    half_mask = jnp.take(my_columns, half_ids // BLOCK, axis=0).astype(jnp.bfloat16)
    regrouped = lax.all_to_all(panel_data, "tm", split_axis=1, concat_axis=0, tiled=True)
    vec_half = jnp.dot((half_mask * regrouped).T, half_weighted, preferred_element_type=jnp.float32)
    group_rows = min(rows_own, BLOCK)
    n_groups = n_time * rows_own // group_rows
    group_gram = jnp.einsum(
        "gnk,gnl->gkl",
        half_weighted.reshape(n_groups, group_rows, width),
        half_load.reshape(n_groups, group_rows, width),
        preferred_element_type=jnp.float32,
    )
    group_block = half_ids.reshape(n_groups, group_rows)[:, 0] // BLOCK
    group_mask = jnp.take(my_columns, group_block, axis=0).astype(jnp.float32)
    info_half = jnp.einsum("gt,gkl->tkl", group_mask, group_gram, precision=HIGHEST)
    info_mat, info_vec = lax.psum((info_half, vec_half), "unit")
    global_step = time_index * steps + jnp.arange(steps, dtype=jnp.int32)
    first_step = (global_step == 0).astype(jnp.float32)
    keep_step = 1.0 - first_step
    last_keep = 1.0 - (global_step == total_time - 1).astype(jnp.float32)
    inv_var = 1.0 / proc_var
    prior_prec = first_step[:, None, None] * identity_mat + keep_step[:, None, None] * jnp.diag(
        inv_var
    )
    eyes = jnp.broadcast_to(identity_mat, info_mat.shape)
    post_cov = chol_apply(jnp.linalg.cholesky(prior_prec + info_mat), eyes)
    shift_vec = jnp.einsum(
        "skl,sl->sk",
        post_cov,
        info_vec + first_step[:, None] * prior_mean[None, :],
        precision=HIGHEST,
    )
    scaled_trans = inv_var[:, None] * transition
    trans_part = keep_step[:, None, None] * jnp.einsum(
        "skl,lm->skm", post_cov, scaled_trans, precision=HIGHEST
    )
    middle = jnp.diag(inv_var)[None] - inv_var[None, :, None] * post_cov * inv_var[None, None, :]
    pressed = jnp.einsum("slm,mn->sln", middle, transition, precision=HIGHEST)
    info_part = keep_step[:, None, None] * jnp.einsum(
        "lk,sln->skn", transition, pressed, precision=HIGHEST
    )
    vec_part = keep_step[:, None] * jnp.einsum(
        "lk,sl->sk", transition, inv_var[None, :] * shift_vec, precision=HIGHEST
    )
    elements = (
        trans_part,
        shift_vec,
        post_cov,
        info_part,
        vec_part,
        jnp.ones((steps,), jnp.float32),
    )
    zero_vec = jnp.zeros((width,), jnp.float32)
    zero_mat = jnp.zeros((width, width), jnp.float32)
    filter_identity = (identity_mat, zero_vec, zero_mat, zero_mat, zero_vec, jnp.float32(0.0))
    local_joined = lax.associative_scan(filter_join, elements)
    filter_total = jax.tree.map(take_last, local_joined)
    before = carried_in(filter_total, "tm", filter_join, filter_identity, False)
    filtered = jax.vmap(filter_join, in_axes=(None, 0))(before, local_joined)
    filt_mean = filtered[1]
    filt_cov = filtered[2]
    moved_cov = jnp.einsum("kl,slm->skm", transition, filt_cov, precision=HIGHEST)
    pred_next = (
        jnp.einsum("skm,nm->skn", moved_cov, transition, precision=HIGHEST)
        + jnp.diag(proc_var)[None]
    )
    gain = (
        jnp.transpose(chol_apply(jnp.linalg.cholesky(pred_next), moved_cov), (0, 2, 1))
        * last_keep[:, None, None]
    )
    moved_mean = jnp.einsum("kl,sl->sk", transition, filt_mean, precision=HIGHEST)
    offset = filt_mean - jnp.einsum("skl,sl->sk", gain, moved_mean, precision=HIGHEST)
    resid_cov = filt_cov - jnp.einsum("skl,slm->skm", gain, moved_cov, precision=HIGHEST)
    smooth_identity = (identity_mat, zero_vec, zero_mat)
    local_suffix = lax.associative_scan(smooth_scan_join, (gain, offset, resid_cov), reverse=True)
    smooth_total = jax.tree.map(take_first, local_suffix)
    after = carried_in(smooth_total, "tm", smooth_scan_join, smooth_identity, True)
    smoothed = jax.vmap(smooth_join, in_axes=(0, None))(local_suffix, after)
    smoothed_mean = smoothed[1]
    smoothed_var = jnp.diagonal(smoothed[2], axis1=1, axis2=2)
    return (smoothed_mean, smoothed_var)


def per_device_any(*arrays):
    fits = arrays[0].shape[1] <= 64 * lax.axis_size("unit") and lax.axis_size("unit") == 2
    return redundant(*arrays) if fits else per_device(*arrays)


def solution(mesh):
    return jax.shard_map(
        per_device_any,
        mesh=mesh,
        in_specs=(P(("grp", "tm", "unit"), None), P("grp", None), P(), P(), P(), P(), P()),
        out_specs=(P(("grp", "tm"), None), P(("grp", "tm"), None)),
        check_vma=False,
    )
```

profile of v0, /device:TPU:0, one launch (start us, length us, event | category | flops | bytes accessed | tf_op | source)
XLA Modules:
  0.0 36.1 jit_solution(7150200964772424130)
XLA Ops:
  0.6 0.5 %collective-permute-start = (bf16[32,64]{1,0:T(8,128)(2,1)}, bf16[32,64]{1,0:T(8,128)(2,1)S(1)}, u32[]{:S(2)}, u32[]{:S(2)}) collective-permute-start(bf16[32,64]{1,0:T(8,128)(2,1)} %param.7), channel_id=1, source_target_pairs={{0,1},{1,0},{2,3},{3,2},{4,5},{5,4},{6,7},{7,6},{8,9},{9,8},{10,11... | collective-permute-start | bytes 12296 | tf_op jit(solution)/shard_map/ppermute | solution.py:847
  1.1 0.1 pad_add_fusion.index_ref
  1.2 0.0 copy-start
  1.2 5.4 %first_sweep.1 = (bf16[4,128,128]{2,1,0:T(8,128)(2,1)S(1)}, f32[128,128]{1,0:T(8,128)S(1)}, bf16[4,64]{1,0:T(4,128)(2,1)S(1)}, f32[2,128,128]{2,1,0:T(8,128)S(1)...) custom-call(s32[4]{0:T(128)S(1)} %pad_add_fusion.index_ref, ...), custom_call_target="tpu_custom_call" | custom-call | flops 20132659200 | bytes 1048576 | tf_op jit(solution)/shard_map/first_sweep/pallas_call | solution.py:600
  6.6 0.0 collective-permute-done
  6.6 0.0 copy-done
  6.6 3.7 %collective-permute-start.1 = (bf16[64,64]{1,0:T(8,128)(2,1)S(1)}, bf16[64,64]{1,0:T(8,128)(2,1)S(1)}, u32[]{:S(2)}, u32[]{:S(2)}) collective-permute-start(bf16[64,64]{1,0:T(8,128)(2,1)S(1)} %pad_maximum_fusion.3), channel_id=1, source_target_pairs={{0,8},{2,10},{4,12},{6,14},{8,0},{10,2},{12,4},{14,6},{1,9},{3,11}... | collective-permute-start | bytes 24584 | tf_op jit(solution)/shard_map/ppermute | solution.py:838
  10.3 3.5 %up_sweep_1.1 = (bf16[8,256,256]{2,1,0:T(8,128)(2,1)S(1)}, bf16[8,256,256]{2,1,0:T(8,128)(2,1)S(1)}, f32[8,128,128]{2,1,0:T(8,128)S(1)}, f32[8,128,128]{2,1,0:T(...) custom-call(s32[4]{0:T(128)S(1)} %pad_add_fusion.index_ref, ...), custom_call_target="tpu_custom_call" | custom-call | flops 20132659200 | bytes 1048576 | tf_op jit(solution)/shard_map/up_sweep_1/pallas_call | solution.py:636
  13.8 0.0 collective-permute-done.1
  13.9 1.6 %collective-permute-start.2 = (bf16[128,64]{1,0:T(8,128)(2,1)S(1)}, bf16[128,64]{1,0:T(8,128)(2,1)S(1)}, u32[]{:S(2)}, u32[]{:S(2)}) collective-permute-start(bf16[128,64]{1,0:T(8,128)(2,1)S(1)} %pad_maximum_fusion.2), channel_id=1, source_target_pairs={{0,4},{2,6},{4,0},{6,2},{8,12},{10,14},{12,8},{14,10},{1,5},{3,7},... | collective-permute-start | bytes 49160 | tf_op jit(solution)/shard_map/ppermute | solution.py:838
  15.5 2.9 %up_sweep_2.1 = (bf16[4,256,256]{2,1,0:T(8,128)(2,1)S(1)}, bf16[4,256,256]{2,1,0:T(8,128)(2,1)S(1)}, f32[4,128,128]{2,1,0:T(8,128)S(1)}, f32[4,128,128]{2,1,0:T(...) custom-call(s32[4]{0:T(128)S(1)} %pad_add_fusion.index_ref, ...), custom_call_target="tpu_custom_call" | custom-call | flops 10066329600 | bytes 1048576 | tf_op jit(solution)/shard_map/up_sweep_2/pallas_call | solution.py:636
  18.4 0.0 collective-permute-done.2
  18.4 1.6 %collective-permute-start.3 = (bf16[256,64]{1,0:T(8,128)(2,1)S(1)}, bf16[256,64]{1,0:T(8,128)(2,1)S(1)}, u32[]{:S(2)}, u32[]{:S(2)}) collective-permute-start(bf16[256,64]{1,0:T(8,128)(2,1)S(1)} %pad_maximum_fusion.1), channel_id=1, source_target_pairs={{0,2},{2,0},{4,6},{6,4},{8,10},{10,8},{12,14},{14,12},{1,3},{3,1},... | collective-permute-start | bytes 98312 | tf_op jit(solution)/shard_map/ppermute | solution.py:838
  20.0 2.3 %up_sweep_3.1 = (bf16[2,256,256]{2,1,0:T(8,128)(2,1)S(1)}, bf16[2,256,256]{2,1,0:T(8,128)(2,1)S(1)}, f32[2,128,128]{2,1,0:T(8,128)S(1)}, f32[2,128,128]{2,1,0:T(...) custom-call(s32[4]{0:T(128)S(1)} %pad_add_fusion.index_ref, ...), custom_call_target="tpu_custom_call" | custom-call | flops 5033164800 | bytes 1048576 | tf_op jit(solution)/shard_map/up_sweep_3/pallas_call | solution.py:636
  22.3 0.4 %collective-permute-done.3 = bf16[256,64]{1,0:T(8,128)(2,1)S(1)} collective-permute-done((bf16[256,64]{1,0:T(8,128)(2,1)S(1)}, bf16[256,64]{1,0:T(8,128)(2,1)S(1)}, u32[]{:S(2)}, u32[]{:S(2)}) %collective-permute-start.3) | collective-permute-done | bytes 32800 | tf_op jit(solution)/shard_map/ppermute | solution.py:838
  22.8 3.3 %up_sweep_4.1 = (bf16[1,256,256]{2,1,0:T(8,128)(2,1)S(1)}, bf16[1,256,256]{2,1,0:T(8,128)(2,1)S(1)}, f32[1,128,128]{2,1,0:T(8,128)S(1)}, f32[1,128,128]{2,1,0:T(...) custom-call(s32[4]{0:T(128)S(1)} %pad_add_fusion.index_ref, ...), custom_call_target="tpu_custom_call" | custom-call | flops 2516582400 | bytes 1048576 | tf_op jit(solution)/shard_map/up_sweep_4/pallas_call | solution.py:636
  26.1 0.0 collective-permute-start.4
  26.1 1.4 %collective-permute-done.4.other_ref = f32[392,128]{1,0:T(8,128)S(1)} collective-permute-done((f32[392,128]{1,0:T(8,128)S(1)}, f32[392,128]{1,0:T(8,128)S(1)}, u32[]{:S(2)}, u32[]{:S(2)}) %collective-permute-start.4) | collective-permute-done | bytes 200736 | tf_op jit(solution)/shard_map/ppermute | solution.py:859
  27.6 6.7 %down_sweep.1 = f32[16,128]{1,0:T(8,128)S(1)} custom-call(s32[4]{0:T(128)S(1)} %pad_add_fusion.index_ref, f32[392,128]{1,0:T(8,128)S(1)} %get-tuple-element.135.own_ref, f32[392,128]{1,0:T(8,128)S(1)} %collective-permute-done.4.other_ref, f32[128,128]{1,0:T(8,128)S(1)} %get-tuple-element.136.end_ref, f32[2,128,128]{2,1,0:T(8,128)S(1)} %get-tuple-element.80.const_ref, ...), custom_call_target="tpu_custom_call" | custom-call | tf_op jit(solution)/shard_map/down_sweep/pallas_call | solution.py:814
  34.3 0.2 collective-permute-start.5
  34.5 1.0 %collective-permute-done.5 = f32[16,128]{1,0:T(8,128)S(1)} collective-permute-done((f32[16,128]{1,0:T(8,128)S(1)}, f32[16,128]{1,0:T(8,128)S(1)}, u32[]{:S(2)}, u32[]{:S(2)}) %collective-permute-start.5) | collective-permute-done | bytes 8224 | tf_op jit(solution)/shard_map/ppermute | solution.py:864
  35.5 0.6 %fusion = (f32[8,128]{1,0:T(8,128)}, f32[8,128]{1,0:T(8,128)}) fusion(f32[16,128]{1,0:T(8,128)S(1)} %broadcast_select_fusion), kind=kLoop, calls=%fused_computation.6 | loop fusion | bytes 16384 | tf_op jit(solution)/shard_map/slice | solution.py:866
  (5 shorter events, 0.1 us)
Async XLA Ops:
  0.6 6.0 %collective-permute-start = (bf16[32,64]{1,0:T(8,128)(2,1)}, bf16[32,64]{1,0:T(8,128)(2,1)S(1)}, u32[]{:S(2)}, u32[]{:S(2)}) collective-permute-start(bf16[32,64]{1,0:T(8,128)(2,1)} %param.7), channel_id=1, source_target_pairs={{0,1},{1,0},{2,3},{3,2},{4,5},{5,4},{6,7},{7,6},{8,9},{9,8},{10,11... | collective-permute-start | bytes 12296 | tf_op jit(solution)/shard_map/ppermute | solution.py:847
  1.2 5.4 %copy-start = (bf16[32,64]{1,0:T(8,128)(2,1)S(1)}, bf16[32,64]{1,0:T(8,128)(2,1)}, u32[]{:S(2)}) copy-start(bf16[32,64]{1,0:T(8,128)(2,1)} %param.7) | copy-start | bytes 12292
  6.6 7.2 %collective-permute-start.1 = (bf16[64,64]{1,0:T(8,128)(2,1)S(1)}, bf16[64,64]{1,0:T(8,128)(2,1)S(1)}, u32[]{:S(2)}, u32[]{:S(2)}) collective-permute-start(bf16[64,64]{1,0:T(8,128)(2,1)S(1)} %pad_maximum_fusion.3), channel_id=1, source_target_pairs={{0,8},{2,10},{4,12},{6,14},{8,0},{10,2},{12,4},{14,6},{1,9},{3,11}... | collective-permute-start | bytes 24584 | tf_op jit(solution)/shard_map/ppermute | solution.py:838
  13.9 4.5 %collective-permute-start.2 = (bf16[128,64]{1,0:T(8,128)(2,1)S(1)}, bf16[128,64]{1,0:T(8,128)(2,1)S(1)}, u32[]{:S(2)}, u32[]{:S(2)}) collective-permute-start(bf16[128,64]{1,0:T(8,128)(2,1)S(1)} %pad_maximum_fusion.2), channel_id=1, source_target_pairs={{0,4},{2,6},{4,0},{6,2},{8,12},{10,14},{12,8},{14,10},{1,5},{3,7},... | collective-permute-start | bytes 49160 | tf_op jit(solution)/shard_map/ppermute | solution.py:838
  18.4 4.3 %collective-permute-start.3 = (bf16[256,64]{1,0:T(8,128)(2,1)S(1)}, bf16[256,64]{1,0:T(8,128)(2,1)S(1)}, u32[]{:S(2)}, u32[]{:S(2)}) collective-permute-start(bf16[256,64]{1,0:T(8,128)(2,1)S(1)} %pad_maximum_fusion.1), channel_id=1, source_target_pairs={{0,2},{2,0},{4,6},{6,4},{8,10},{10,8},{12,14},{14,12},{1,3},{3,1},... | collective-permute-start | bytes 98312 | tf_op jit(solution)/shard_map/ppermute | solution.py:838
  26.1 1.5 %collective-permute-start.4 = (f32[392,128]{1,0:T(8,128)S(1)}, f32[392,128]{1,0:T(8,128)S(1)}, u32[]{:S(2)}, u32[]{:S(2)}) collective-permute-start(f32[392,128]{1,0:T(8,128)S(1)} %get-tuple-element.135.own_ref), channel_id=1, source_target_pairs={{0,1},{1,0},{2,3},{3,2},{4,5},{5,4},{6,7},{7,6},{8,9},{9,8},{10,11... | collective-permute-start | bytes 602120 | tf_op jit(solution)/shard_map/ppermute | solution.py:859
  34.3 1.2 %collective-permute-start.5 = (f32[16,128]{1,0:T(8,128)S(1)}, f32[16,128]{1,0:T(8,128)S(1)}, u32[]{:S(2)}, u32[]{:S(2)}) collective-permute-start(f32[16,128]{1,0:T(8,128)S(1)} %down_sweep.1), channel_id=1, source_target_pairs={{0,1},{1,0},{2,3},{3,2},{4,5},{5,4},{6,7},{7,6},{8,9},{9,8},{10,11... | collective-permute-start | bytes 24584 | tf_op jit(solution)/shard_map/ppermute | solution.py:864
where the time goes:
time: 36.3 us; the launch traced here: 36.1 us
  Pallas kernels  24.1 us (66%)
  starting transfers between devices  7.6 us (21%)
  waiting for transfers between devices  2.91 us (8%)
  between operations  0.73 us (2%)
  local copies, waits for them, and re-layouts  0.61 us (2%)
    pallas_call x4, Pallas kernels, up_sweep(): pl.pallas_call(functools.partial(up_kernel, joins, half, steps, rows_own)...  12 us
    ppermute x3, starting transfers between devices, swapped(): return lax.ppermute(value, 'tm', [(k, k ^ other) for k in range(n_time)])  6.88 us
    pallas_call x1, Pallas kernels, down_sweep(): pl.pallas_call(functools.partial(down_kernel, steps), out_shape=jax.Shape...  6.7 us
    pallas_call x1, Pallas kernels, first_sweep(): pl.pallas_call(functools.partial(first_kernel, half), out_shape=outs, in_...  5.37 us
    ppermute x1, waiting for transfers between devices, redundant(): other = lax.ppermute(message, 'unit', swap)  1.44 us
    ppermute x1, waiting for transfers between devices, redundant(): theirs = lax.ppermute(mine, 'unit', swap)  1.03 us
  transfers between devices with their start and end apart: 6, of which 3 were waited for; matrix products, arithmetic and copies ran while one was open for 0% of the time, Pallas kernels for 39%

commit v1 on v0

--- a/solution.py
+++ b/solution.py
@@ -111,9 +111,11 @@
         resid[k] = fine[k]
         guess[k] = guess[k] + mm(guess[k].astype(bf16), fine[k].astype(bf16))
         sides[k] = (guess[k], None)
-    worst = squares(resid[0])
-    for e in resid[1:]:
-        worst = jnp.maximum(worst, squares(e))
+    sizes = [squares(e) for e in resid]
+    sizes = [jnp.where(size < 1e6, size, 1e6) for size in sizes]
+    worst = sizes[0]
+    for size in sizes[1:]:
+        worst = jnp.maximum(worst, size)
     return guess, sides, worst
 
 
@@ -692,12 +694,14 @@
         z = mm3(u, cov0)
         kept = mm3(p, cov0)
         results = []
-        in_turns(conditioning(entries, [scale for _, scale in extra], inverses, results), beside)
+        work = conditioning(entries, [scale for _, scale in extra], inverses, results)
+        info_z = mm3(jnp.transpose(z), end)
+        _, (side,) = invert([(last, bounds_at(JOIN_BOUNDS, 0), False)], eye, fast, acc_ref, True, work)
+        for _ in work:
+            pass
         for slot, result in enumerate(results):
             for ref, value in zip((gt_ref, cond_ref, shift_ref), result):
                 ref[slot] = value
-        info_z = mm3(jnp.transpose(z), end)
-        _, (side,) = invert([(last, bounds_at(JOIN_BOUNDS, 0), False)], eye, fast, acc_ref, True)
         top_ref[0], top_ref[1] = inverse_times(side, cov, eye), inverse_times(side, z, eye)
         top_ref[2] = kept - mm3(info_z, top_ref[1])
         top_ref[3] = p
@@ -1064,7 +1068,8 @@
 
 
 def per_device_any(*arrays):
-    fits = arrays[0].shape[1] <= 64 * lax.axis_size("unit") and lax.axis_size("unit") == 2
+    half = arrays[0].shape[1] // 2
+    fits = lax.axis_size("unit") == 2 and half in (32, 64) and arrays[4].shape[0] == WIDTH
     return redundant(*arrays) if fits else per_device(*arrays)
 
 

time: 36.3 us -> 36 us (level)
  no operation moved by 1% of the time
where the time goes in v1:
time: 36 us; the launch traced here: 35.8 us
  Pallas kernels  23.8 us (66%)
  starting transfers between devices  7.6 us (21%)
  waiting for transfers between devices  2.91 us (8%)
  between operations  0.73 us (2%)
  local copies, waits for them, and re-layouts  0.61 us (2%)
    pallas_call x4, Pallas kernels, up_sweep(): pl.pallas_call(functools.partial(up_kernel, joins, half, steps, rows_own)...  12 us
    ppermute x3, starting transfers between devices, swapped(): return lax.ppermute(value, 'tm', [(k, k ^ other) for k in range(n_time)])  6.88 us
    pallas_call x1, Pallas kernels, down_sweep(): pl.pallas_call(functools.partial(down_kernel, steps), out_shape=jax.Shape...  6.4 us
    pallas_call x1, Pallas kernels, first_sweep(): pl.pallas_call(functools.partial(first_kernel, half), out_shape=outs, in_...  5.37 us
    ppermute x1, waiting for transfers between devices, redundant(): other = lax.ppermute(message, 'unit', swap)  1.44 us
    ppermute x1, waiting for transfers between devices, redundant(): theirs = lax.ppermute(mine, 'unit', swap)  1.03 us
  transfers between devices with their start and end apart: 6, of which 3 were waited for; matrix products, arithmetic and copies ran while one was open for 0% of the time, Pallas kernels for 39%

profile of v1, /device:TPU:0, one launch (start us, length us, event | category | flops | bytes accessed | tf_op | source)
XLA Modules:
  0.0 35.8 jit_solution(10740344892890292065)
XLA Ops:
  0.6 0.5 %collective-permute-start = (bf16[32,64]{1,0:T(8,128)(2,1)}, bf16[32,64]{1,0:T(8,128)(2,1)S(1)}, u32[]{:S(2)}, u32[]{:S(2)}) collective-permute-start(bf16[32,64]{1,0:T(8,128)(2,1)} %param.7), channel_id=1, source_target_pairs={{0,1},{1,0},{2,3},{3,2},{4,5},{5,4},{6,7},{7,6},{8,9},{9,8},{10,11... | collective-permute-start | bytes 12296 | tf_op jit(solution)/shard_map/ppermute | solution.py:851
  1.1 0.1 pad_add_fusion.index_ref
  1.2 0.0 copy-start
  1.2 5.4 %first_sweep.1 = (bf16[4,128,128]{2,1,0:T(8,128)(2,1)S(1)}, f32[128,128]{1,0:T(8,128)S(1)}, bf16[4,64]{1,0:T(4,128)(2,1)S(1)}, f32[2,128,128]{2,1,0:T(8,128)S(1)...) custom-call(s32[4]{0:T(128)S(1)} %pad_add_fusion.index_ref, ...), custom_call_target="tpu_custom_call" | custom-call | flops 20132659200 | bytes 1048576 | tf_op jit(solution)/shard_map/first_sweep/pallas_call | solution.py:602
  6.6 0.0 collective-permute-done
  6.6 0.0 copy-done
  6.6 3.7 %collective-permute-start.1 = (bf16[64,64]{1,0:T(8,128)(2,1)S(1)}, bf16[64,64]{1,0:T(8,128)(2,1)S(1)}, u32[]{:S(2)}, u32[]{:S(2)}) collective-permute-start(bf16[64,64]{1,0:T(8,128)(2,1)S(1)} %pad_maximum_fusion.3), channel_id=1, source_target_pairs={{0,8},{2,10},{4,12},{6,14},{8,0},{10,2},{12,4},{14,6},{1,9},{3,11}... | collective-permute-start | bytes 24584 | tf_op jit(solution)/shard_map/ppermute | solution.py:842
  10.3 3.5 %up_sweep_1.1 = (bf16[8,256,256]{2,1,0:T(8,128)(2,1)S(1)}, bf16[8,256,256]{2,1,0:T(8,128)(2,1)S(1)}, f32[8,128,128]{2,1,0:T(8,128)S(1)}, f32[8,128,128]{2,1,0:T(...) custom-call(s32[4]{0:T(128)S(1)} %pad_add_fusion.index_ref, ...), custom_call_target="tpu_custom_call" | custom-call | flops 20132659200 | bytes 1048576 | tf_op jit(solution)/shard_map/up_sweep_1/pallas_call | solution.py:638
  13.8 0.0 collective-permute-done.1
  13.9 1.6 %collective-permute-start.2 = (bf16[128,64]{1,0:T(8,128)(2,1)S(1)}, bf16[128,64]{1,0:T(8,128)(2,1)S(1)}, u32[]{:S(2)}, u32[]{:S(2)}) collective-permute-start(bf16[128,64]{1,0:T(8,128)(2,1)S(1)} %pad_maximum_fusion.2), channel_id=1, source_target_pairs={{0,4},{2,6},{4,0},{6,2},{8,12},{10,14},{12,8},{14,10},{1,5},{3,7},... | collective-permute-start | bytes 49160 | tf_op jit(solution)/shard_map/ppermute | solution.py:842
  15.5 2.9 %up_sweep_2.1 = (bf16[4,256,256]{2,1,0:T(8,128)(2,1)S(1)}, bf16[4,256,256]{2,1,0:T(8,128)(2,1)S(1)}, f32[4,128,128]{2,1,0:T(8,128)S(1)}, f32[4,128,128]{2,1,0:T(...) custom-call(s32[4]{0:T(128)S(1)} %pad_add_fusion.index_ref, ...), custom_call_target="tpu_custom_call" | custom-call | flops 10066329600 | bytes 1048576 | tf_op jit(solution)/shard_map/up_sweep_2/pallas_call | solution.py:638
  18.4 0.0 collective-permute-done.2
  18.4 1.6 %collective-permute-start.3 = (bf16[256,64]{1,0:T(8,128)(2,1)S(1)}, bf16[256,64]{1,0:T(8,128)(2,1)S(1)}, u32[]{:S(2)}, u32[]{:S(2)}) collective-permute-start(bf16[256,64]{1,0:T(8,128)(2,1)S(1)} %pad_maximum_fusion.1), channel_id=1, source_target_pairs={{0,2},{2,0},{4,6},{6,4},{8,10},{10,8},{12,14},{14,12},{1,3},{3,1},... | collective-permute-start | bytes 98312 | tf_op jit(solution)/shard_map/ppermute | solution.py:842
  20.0 2.3 %up_sweep_3.1 = (bf16[2,256,256]{2,1,0:T(8,128)(2,1)S(1)}, bf16[2,256,256]{2,1,0:T(8,128)(2,1)S(1)}, f32[2,128,128]{2,1,0:T(8,128)S(1)}, f32[2,128,128]{2,1,0:T(...) custom-call(s32[4]{0:T(128)S(1)} %pad_add_fusion.index_ref, ...), custom_call_target="tpu_custom_call" | custom-call | flops 5033164800 | bytes 1048576 | tf_op jit(solution)/shard_map/up_sweep_3/pallas_call | solution.py:638
  22.3 0.4 %collective-permute-done.3 = bf16[256,64]{1,0:T(8,128)(2,1)S(1)} collective-permute-done((bf16[256,64]{1,0:T(8,128)(2,1)S(1)}, bf16[256,64]{1,0:T(8,128)(2,1)S(1)}, u32[]{:S(2)}, u32[]{:S(2)}) %collective-permute-start.3) | collective-permute-done | bytes 32800 | tf_op jit(solution)/shard_map/ppermute | solution.py:842
  22.8 3.3 %up_sweep_4.1 = (bf16[1,256,256]{2,1,0:T(8,128)(2,1)S(1)}, bf16[1,256,256]{2,1,0:T(8,128)(2,1)S(1)}, f32[1,128,128]{2,1,0:T(8,128)S(1)}, f32[1,128,128]{2,1,0:T(...) custom-call(s32[4]{0:T(128)S(1)} %pad_add_fusion.index_ref, ...), custom_call_target="tpu_custom_call" | custom-call | flops 2516582400 | bytes 1048576 | tf_op jit(solution)/shard_map/up_sweep_4/pallas_call | solution.py:638
  26.1 0.0 collective-permute-start.4
  26.1 1.4 %collective-permute-done.4.other_ref = f32[392,128]{1,0:T(8,128)S(1)} collective-permute-done((f32[392,128]{1,0:T(8,128)S(1)}, f32[392,128]{1,0:T(8,128)S(1)}, u32[]{:S(2)}, u32[]{:S(2)}) %collective-permute-start.4) | collective-permute-done | bytes 200736 | tf_op jit(solution)/shard_map/ppermute | solution.py:863
  27.6 6.4 %down_sweep.1 = f32[16,128]{1,0:T(8,128)S(1)} custom-call(s32[4]{0:T(128)S(1)} %pad_add_fusion.index_ref, f32[392,128]{1,0:T(8,128)S(1)} %get-tuple-element.135.own_ref, f32[392,128]{1,0:T(8,128)S(1)} %collective-permute-done.4.other_ref, f32[128,128]{1,0:T(8,128)S(1)} %get-tuple-element.136.end_ref, f32[2,128,128]{2,1,0:T(8,128)S(1)} %get-tuple-element.80.const_ref, ...), custom_call_target="tpu_custom_call" | custom-call | tf_op jit(solution)/shard_map/down_sweep/pallas_call | solution.py:818
  34.0 0.2 collective-permute-start.5
  34.2 1.0 %collective-permute-done.5 = f32[16,128]{1,0:T(8,128)S(1)} collective-permute-done((f32[16,128]{1,0:T(8,128)S(1)}, f32[16,128]{1,0:T(8,128)S(1)}, u32[]{:S(2)}, u32[]{:S(2)}) %collective-permute-start.5) | collective-permute-done | bytes 8224 | tf_op jit(solution)/shard_map/ppermute | solution.py:868
  35.2 0.6 %fusion = (f32[8,128]{1,0:T(8,128)}, f32[8,128]{1,0:T(8,128)}) fusion(f32[16,128]{1,0:T(8,128)S(1)} %broadcast_select_fusion), kind=kLoop, calls=%fused_computation.6 | loop fusion | bytes 16384 | tf_op jit(solution)/shard_map/slice | solution.py:870
  (5 shorter events, 0.1 us)
Async XLA Ops:
  0.6 6.0 %collective-permute-start = (bf16[32,64]{1,0:T(8,128)(2,1)}, bf16[32,64]{1,0:T(8,128)(2,1)S(1)}, u32[]{:S(2)}, u32[]{:S(2)}) collective-permute-start(bf16[32,64]{1,0:T(8,128)(2,1)} %param.7), channel_id=1, source_target_pairs={{0,1},{1,0},{2,3},{3,2},{4,5},{5,4},{6,7},{7,6},{8,9},{9,8},{10,11... | collective-permute-start | bytes 12296 | tf_op jit(solution)/shard_map/ppermute | solution.py:851
  1.2 5.4 %copy-start = (bf16[32,64]{1,0:T(8,128)(2,1)S(1)}, bf16[32,64]{1,0:T(8,128)(2,1)}, u32[]{:S(2)}) copy-start(bf16[32,64]{1,0:T(8,128)(2,1)} %param.7) | copy-start | bytes 12292
  6.6 7.2 %collective-permute-start.1 = (bf16[64,64]{1,0:T(8,128)(2,1)S(1)}, bf16[64,64]{1,0:T(8,128)(2,1)S(1)}, u32[]{:S(2)}, u32[]{:S(2)}) collective-permute-start(bf16[64,64]{1,0:T(8,128)(2,1)S(1)} %pad_maximum_fusion.3), channel_id=1, source_target_pairs={{0,8},{2,10},{4,12},{6,14},{8,0},{10,2},{12,4},{14,6},{1,9},{3,11}... | collective-permute-start | bytes 24584 | tf_op jit(solution)/shard_map/ppermute | solution.py:842
  13.9 4.5 %collective-permute-start.2 = (bf16[128,64]{1,0:T(8,128)(2,1)S(1)}, bf16[128,64]{1,0:T(8,128)(2,1)S(1)}, u32[]{:S(2)}, u32[]{:S(2)}) collective-permute-start(bf16[128,64]{1,0:T(8,128)(2,1)S(1)} %pad_maximum_fusion.2), channel_id=1, source_target_pairs={{0,4},{2,6},{4,0},{6,2},{8,12},{10,14},{12,8},{14,10},{1,5},{3,7},... | collective-permute-start | bytes 49160 | tf_op jit(solution)/shard_map/ppermute | solution.py:842
  18.4 4.3 %collective-permute-start.3 = (bf16[256,64]{1,0:T(8,128)(2,1)S(1)}, bf16[256,64]{1,0:T(8,128)(2,1)S(1)}, u32[]{:S(2)}, u32[]{:S(2)}) collective-permute-start(bf16[256,64]{1,0:T(8,128)(2,1)S(1)} %pad_maximum_fusion.1), channel_id=1, source_target_pairs={{0,2},{2,0},{4,6},{6,4},{8,10},{10,8},{12,14},{14,12},{1,3},{3,1},... | collective-permute-start | bytes 98312 | tf_op jit(solution)/shard_map/ppermute | solution.py:842
  26.1 1.5 %collective-permute-start.4 = (f32[392,128]{1,0:T(8,128)S(1)}, f32[392,128]{1,0:T(8,128)S(1)}, u32[]{:S(2)}, u32[]{:S(2)}) collective-permute-start(f32[392,128]{1,0:T(8,128)S(1)} %get-tuple-element.135.own_ref), channel_id=1, source_target_pairs={{0,1},{1,0},{2,3},{3,2},{4,5},{5,4},{6,7},{7,6},{8,9},{9,8},{10,11... | collective-permute-start | bytes 602120 | tf_op jit(solution)/shard_map/ppermute | solution.py:863
  34.0 1.2 %collective-permute-start.5 = (f32[16,128]{1,0:T(8,128)S(1)}, f32[16,128]{1,0:T(8,128)S(1)}, u32[]{:S(2)}, u32[]{:S(2)}) collective-permute-start(f32[16,128]{1,0:T(8,128)S(1)} %down_sweep.1), channel_id=1, source_target_pairs={{0,1},{1,0},{2,3},{3,2},{4,5},{5,4},{6,7},{7,6},{8,9},{9,8},{10,11... | collective-permute-start | bytes 24584 | tf_op jit(solution)/shard_map/ppermute | solution.py:868

commit v2 on v1

--- a/solution.py
+++ b/solution.py
@@ -111,7 +111,7 @@
         resid[k] = fine[k]
         guess[k] = guess[k] + mm(guess[k].astype(bf16), fine[k].astype(bf16))
         sides[k] = (guess[k], None)
-    sizes = [squares(e) for e in resid]
+    sizes = [jnp.sum(squares(e), keepdims=True) for e in resid]
     sizes = [jnp.where(size < 1e6, size, 1e6) for size in sizes]
     worst = sizes[0]
     for size in sizes[1:]:
@@ -202,7 +202,7 @@
 
 def condition_item(level, entry, eye):
     mat, scale = scaled(entry["c"], eye)
-    return (mat, bounds_at(COV_BOUNDS, level), level > 2), scale
+    return (mat, bounds_at(COV_BOUNDS, level), level > 3), scale
 
 
 def conditioning(entries, scales, inverses, results):
@@ -356,7 +356,7 @@
 def checked(sweep, acc_ref, **beside):
     acc_ref[...] = jnp.zeros((8, WIDTH), f32)
     sweep(True, **beside)
-    worst = jnp.sum(acc_ref[...])
+    worst = jnp.max(acc_ref[...])
 
     @pl.when(jnp.logical_not(worst <= RESIDUAL_MAX))
     def _():

time: 36 us -> 35.7 us (level)
  transfers between devices with their start and end apart: 6 -> 6, of which waited for: 3 -> 3; matrix products, arithmetic and copies ran while one was open for 0% -> 0% of each run, Pallas kernels for 39% -> 40%
where the time goes in v2:
time: 35.7 us; the launch traced here: 35.6 us
  Pallas kernels  23.6 us (66%)
  starting transfers between devices  7.61 us (21%)
  waiting for transfers between devices  2.89 us (8%)
  between operations  0.73 us (2%)
  local copies, waits for them, and re-layouts  0.61 us (2%)
    pallas_call x4, Pallas kernels, up_sweep(): pl.pallas_call(functools.partial(up_kernel, joins, half, steps, rows_own)...  11.7 us
    ppermute x3, starting transfers between devices, swapped(): return lax.ppermute(value, 'tm', [(k, k ^ other) for k in range(n_time)])  6.88 us
    pallas_call x1, Pallas kernels, down_sweep(): pl.pallas_call(functools.partial(down_kernel, steps), out_shape=jax.Shape...  6.43 us
    pallas_call x1, Pallas kernels, first_sweep(): pl.pallas_call(functools.partial(first_kernel, half), out_shape=outs, in_...  5.43 us
    ppermute x1, waiting for transfers between devices, redundant(): other = lax.ppermute(message, 'unit', swap)  1.44 us
    ppermute x1, waiting for transfers between devices, redundant(): theirs = lax.ppermute(mine, 'unit', swap)  1.03 us
  transfers between devices with their start and end apart: 6, of which 3 were waited for; matrix products, arithmetic and copies ran while one was open for 0% of the time, Pallas kernels for 40%

profile of v2, /device:TPU:0, one launch (start us, length us, event | category | flops | bytes accessed | tf_op | source)
XLA Modules:
  0.0 35.6 jit_solution(7046836340506455154)
XLA Ops:
  0.6 0.5 %collective-permute-start = (bf16[32,64]{1,0:T(8,128)(2,1)}, bf16[32,64]{1,0:T(8,128)(2,1)S(1)}, u32[]{:S(2)}, u32[]{:S(2)}) collective-permute-start(bf16[32,64]{1,0:T(8,128)(2,1)} %param.7), channel_id=1, source_target_pairs={{0,1},{1,0},{2,3},{3,2},{4,5},{5,4},{6,7},{7,6},{8,9},{9,8},{10,11... | collective-permute-start | bytes 12296 | tf_op jit(solution)/shard_map/ppermute | solution.py:851
  1.1 0.1 pad_add_fusion.index_ref
  1.2 0.0 copy-start
  1.2 5.4 %first_sweep.1 = (bf16[4,128,128]{2,1,0:T(8,128)(2,1)S(1)}, f32[128,128]{1,0:T(8,128)S(1)}, bf16[4,64]{1,0:T(4,128)(2,1)S(1)}, f32[2,128,128]{2,1,0:T(8,128)S(1)...) custom-call(s32[4]{0:T(128)S(1)} %pad_add_fusion.index_ref, ...), custom_call_target="tpu_custom_call" | custom-call | flops 20132659200 | bytes 1048576 | tf_op jit(solution)/shard_map/first_sweep/pallas_call | solution.py:602
  6.7 0.0 collective-permute-done
  6.7 0.0 copy-done
  6.7 3.7 %collective-permute-start.1 = (bf16[64,64]{1,0:T(8,128)(2,1)S(1)}, bf16[64,64]{1,0:T(8,128)(2,1)S(1)}, u32[]{:S(2)}, u32[]{:S(2)}) collective-permute-start(bf16[64,64]{1,0:T(8,128)(2,1)S(1)} %pad_maximum_fusion.3), channel_id=1, source_target_pairs={{0,8},{2,10},{4,12},{6,14},{8,0},{10,2},{12,4},{14,6},{1,9},{3,11}... | collective-permute-start | bytes 24584 | tf_op jit(solution)/shard_map/ppermute | solution.py:842
  10.4 3.5 %up_sweep_1.1 = (bf16[8,256,256]{2,1,0:T(8,128)(2,1)S(1)}, bf16[8,256,256]{2,1,0:T(8,128)(2,1)S(1)}, f32[8,128,128]{2,1,0:T(8,128)S(1)}, f32[8,128,128]{2,1,0:T(...) custom-call(s32[4]{0:T(128)S(1)} %pad_add_fusion.index_ref, ...), custom_call_target="tpu_custom_call" | custom-call | flops 20132659200 | bytes 1048576 | tf_op jit(solution)/shard_map/up_sweep_1/pallas_call | solution.py:638
  13.9 0.0 collective-permute-done.1
  13.9 1.6 %collective-permute-start.2 = (bf16[128,64]{1,0:T(8,128)(2,1)S(1)}, bf16[128,64]{1,0:T(8,128)(2,1)S(1)}, u32[]{:S(2)}, u32[]{:S(2)}) collective-permute-start(bf16[128,64]{1,0:T(8,128)(2,1)S(1)} %pad_maximum_fusion.2), channel_id=1, source_target_pairs={{0,4},{2,6},{4,0},{6,2},{8,12},{10,14},{12,8},{14,10},{1,5},{3,7},... | collective-permute-start | bytes 49160 | tf_op jit(solution)/shard_map/ppermute | solution.py:842
  15.6 2.9 %up_sweep_2.1 = (bf16[4,256,256]{2,1,0:T(8,128)(2,1)S(1)}, bf16[4,256,256]{2,1,0:T(8,128)(2,1)S(1)}, f32[4,128,128]{2,1,0:T(8,128)S(1)}, f32[4,128,128]{2,1,0:T(...) custom-call(s32[4]{0:T(128)S(1)} %pad_add_fusion.index_ref, ...), custom_call_target="tpu_custom_call" | custom-call | flops 10066329600 | bytes 1048576 | tf_op jit(solution)/shard_map/up_sweep_2/pallas_call | solution.py:638
  18.4 0.0 collective-permute-done.2
  18.5 1.6 %collective-permute-start.3 = (bf16[256,64]{1,0:T(8,128)(2,1)S(1)}, bf16[256,64]{1,0:T(8,128)(2,1)S(1)}, u32[]{:S(2)}, u32[]{:S(2)}) collective-permute-start(bf16[256,64]{1,0:T(8,128)(2,1)S(1)} %pad_maximum_fusion.1), channel_id=1, source_target_pairs={{0,2},{2,0},{4,6},{6,4},{8,10},{10,8},{12,14},{14,12},{1,3},{3,1},... | collective-permute-start | bytes 98312 | tf_op jit(solution)/shard_map/ppermute | solution.py:842
  20.0 2.4 %up_sweep_3.1 = (bf16[2,256,256]{2,1,0:T(8,128)(2,1)S(1)}, bf16[2,256,256]{2,1,0:T(8,128)(2,1)S(1)}, f32[2,128,128]{2,1,0:T(8,128)S(1)}, f32[2,128,128]{2,1,0:T(...) custom-call(s32[4]{0:T(128)S(1)} %pad_add_fusion.index_ref, ...), custom_call_target="tpu_custom_call" | custom-call | flops 5033164800 | bytes 1048576 | tf_op jit(solution)/shard_map/up_sweep_3/pallas_call | solution.py:638
  22.4 0.4 %collective-permute-done.3 = bf16[256,64]{1,0:T(8,128)(2,1)S(1)} collective-permute-done((bf16[256,64]{1,0:T(8,128)(2,1)S(1)}, bf16[256,64]{1,0:T(8,128)(2,1)S(1)}, u32[]{:S(2)}, u32[]{:S(2)}) %collective-permute-start.3) | collective-permute-done | bytes 32800 | tf_op jit(solution)/shard_map/ppermute | solution.py:842
  22.8 3.0 %up_sweep_4.1 = (bf16[1,256,256]{2,1,0:T(8,128)(2,1)S(1)}, bf16[1,256,256]{2,1,0:T(8,128)(2,1)S(1)}, f32[1,128,128]{2,1,0:T(8,128)S(1)}, f32[1,128,128]{2,1,0:T(...) custom-call(s32[4]{0:T(128)S(1)} %pad_add_fusion.index_ref, ...), custom_call_target="tpu_custom_call" | custom-call | flops 2516582400 | bytes 1048576 | tf_op jit(solution)/shard_map/up_sweep_4/pallas_call | solution.py:638
  25.8 0.0 collective-permute-start.4
  25.9 1.4 %collective-permute-done.4.other_ref = f32[392,128]{1,0:T(8,128)S(1)} collective-permute-done((f32[392,128]{1,0:T(8,128)S(1)}, f32[392,128]{1,0:T(8,128)S(1)}, u32[]{:S(2)}, u32[]{:S(2)}) %collective-permute-start.4) | collective-permute-done | bytes 200736 | tf_op jit(solution)/shard_map/ppermute | solution.py:863
  27.3 6.4 %down_sweep.1 = f32[16,128]{1,0:T(8,128)S(1)} custom-call(s32[4]{0:T(128)S(1)} %pad_add_fusion.index_ref, f32[392,128]{1,0:T(8,128)S(1)} %get-tuple-element.135.own_ref, f32[392,128]{1,0:T(8,128)S(1)} %collective-permute-done.4.other_ref, f32[128,128]{1,0:T(8,128)S(1)} %get-tuple-element.136.end_ref, f32[2,128,128]{2,1,0:T(8,128)S(1)} %get-tuple-element.80.const_ref, ...), custom_call_target="tpu_custom_call" | custom-call | tf_op jit(solution)/shard_map/down_sweep/pallas_call | solution.py:818
  33.7 0.2 collective-permute-start.5
  33.9 1.0 %collective-permute-done.5 = f32[16,128]{1,0:T(8,128)S(1)} collective-permute-done((f32[16,128]{1,0:T(8,128)S(1)}, f32[16,128]{1,0:T(8,128)S(1)}, u32[]{:S(2)}, u32[]{:S(2)}) %collective-permute-start.5) | collective-permute-done | bytes 8224 | tf_op jit(solution)/shard_map/ppermute | solution.py:868
  35.0 0.6 %fusion = (f32[8,128]{1,0:T(8,128)}, f32[8,128]{1,0:T(8,128)}) fusion(f32[16,128]{1,0:T(8,128)S(1)} %broadcast_select_fusion), kind=kLoop, calls=%fused_computation.6 | loop fusion | bytes 16384 | tf_op jit(solution)/shard_map/slice | solution.py:870
  (5 shorter events, 0.1 us)
Async XLA Ops:
  0.6 6.0 %collective-permute-start = (bf16[32,64]{1,0:T(8,128)(2,1)}, bf16[32,64]{1,0:T(8,128)(2,1)S(1)}, u32[]{:S(2)}, u32[]{:S(2)}) collective-permute-start(bf16[32,64]{1,0:T(8,128)(2,1)} %param.7), channel_id=1, source_target_pairs={{0,1},{1,0},{2,3},{3,2},{4,5},{5,4},{6,7},{7,6},{8,9},{9,8},{10,11... | collective-permute-start | bytes 12296 | tf_op jit(solution)/shard_map/ppermute | solution.py:851
  1.2 5.4 %copy-start = (bf16[32,64]{1,0:T(8,128)(2,1)S(1)}, bf16[32,64]{1,0:T(8,128)(2,1)}, u32[]{:S(2)}) copy-start(bf16[32,64]{1,0:T(8,128)(2,1)} %param.7) | copy-start | bytes 12292
  6.7 7.2 %collective-permute-start.1 = (bf16[64,64]{1,0:T(8,128)(2,1)S(1)}, bf16[64,64]{1,0:T(8,128)(2,1)S(1)}, u32[]{:S(2)}, u32[]{:S(2)}) collective-permute-start(bf16[64,64]{1,0:T(8,128)(2,1)S(1)} %pad_maximum_fusion.3), channel_id=1, source_target_pairs={{0,8},{2,10},{4,12},{6,14},{8,0},{10,2},{12,4},{14,6},{1,9},{3,11}... | collective-permute-start | bytes 24584 | tf_op jit(solution)/shard_map/ppermute | solution.py:842
  13.9 4.5 %collective-permute-start.2 = (bf16[128,64]{1,0:T(8,128)(2,1)S(1)}, bf16[128,64]{1,0:T(8,128)(2,1)S(1)}, u32[]{:S(2)}, u32[]{:S(2)}) collective-permute-start(bf16[128,64]{1,0:T(8,128)(2,1)S(1)} %pad_maximum_fusion.2), channel_id=1, source_target_pairs={{0,4},{2,6},{4,0},{6,2},{8,12},{10,14},{12,8},{14,10},{1,5},{3,7},... | collective-permute-start | bytes 49160 | tf_op jit(solution)/shard_map/ppermute | solution.py:842
  18.5 4.3 %collective-permute-start.3 = (bf16[256,64]{1,0:T(8,128)(2,1)S(1)}, bf16[256,64]{1,0:T(8,128)(2,1)S(1)}, u32[]{:S(2)}, u32[]{:S(2)}) collective-permute-start(bf16[256,64]{1,0:T(8,128)(2,1)S(1)} %pad_maximum_fusion.1), channel_id=1, source_target_pairs={{0,2},{2,0},{4,6},{6,4},{8,10},{10,8},{12,14},{14,12},{1,3},{3,1},... | collective-permute-start | bytes 98312 | tf_op jit(solution)/shard_map/ppermute | solution.py:842
  25.8 1.5 %collective-permute-start.4 = (f32[392,128]{1,0:T(8,128)S(1)}, f32[392,128]{1,0:T(8,128)S(1)}, u32[]{:S(2)}, u32[]{:S(2)}) collective-permute-start(f32[392,128]{1,0:T(8,128)S(1)} %get-tuple-element.135.own_ref), channel_id=1, source_target_pairs={{0,1},{1,0},{2,3},{3,2},{4,5},{5,4},{6,7},{7,6},{8,9},{9,8},{10,11... | collective-permute-start | bytes 602120 | tf_op jit(solution)/shard_map/ppermute | solution.py:863
  33.7 1.2 %collective-permute-start.5 = (f32[16,128]{1,0:T(8,128)S(1)}, f32[16,128]{1,0:T(8,128)S(1)}, u32[]{:S(2)}, u32[]{:S(2)}) collective-permute-start(f32[16,128]{1,0:T(8,128)S(1)} %down_sweep.1), channel_id=1, source_target_pairs={{0,1},{1,0},{2,3},{3,2},{4,5},{5,4},{6,7},{7,6},{8,9},{9,8},{10,11... | collective-permute-start | bytes 24584 | tf_op jit(solution)/shard_map/ppermute | solution.py:868
